TPU v7x, 128 devices: a whole 4x4x4 slice. The times are simulated.
128 devices in a mesh: rows: 32 (over x, z, core), units: 4 (over y).
Axes of the slice: x: 4, y: 4, z: 4, core: 2. Of those that a mesh axis runs over, the one named last changes fastest.
Arguments:
- residuals: bfloat16 [524288, 2048], P(('rows', 'units')), may hold values from -24 to 24
- loadings: bfloat16 [524288, 256], P(('rows', 'units')), may hold values from -6 to 6
- zero_points: bfloat16 [1024, 2048], P('units'), may hold values from -0.375 to 0.375
- sketch_matrix: bfloat16 [2048, 256], replicated, may hold values from -0.125 to 0.125
- use_lists: int32 [4096, 4], P(('rows', 'units')), may hold values from 0 to 15, all different within a row
Outputs:
- star_basis: float32 [524288, 256], P(('rows', 'units'))
- bin_modes: float32 [2048, 256], P(('rows', 'units'))
Inputs may be any that keep to these rules, and one draw needn't show every extreme that they name: `use_lists`: each row names 4 different groups; every group is named by some row.
All inputs are finite; a program needn't handle non-finite values.
Results may differ from a plain program's by a relative error of at most 0.003.
Values may be sent and summed in bfloat16 or wider, within the bound.
No kernel may reach another device: no remote copies, remote signals or barrier semaphores. Data moves between devices by JAX's collectives and lax.ppermute only.
A program may use at most 192 MiB of HBM per device.

v0:
```python
import jax
import jax.numpy as jnp
from jax import lax
from jax.sharding import PartitionSpec as P

GROUP = 64
USES = 4
BLOCK_STARS = 128


def on_device(residuals, loadings, zero_points, sketch_matrix, use_lists):
    gathered = lax.all_gather(zero_points, "units", axis=0, tiled=True)
    local_rows, width_bins = residuals.shape
    group_count = gathered.shape[0] // GROUP
    block_count = use_lists.shape[0]
    tables = gathered.reshape(group_count, GROUP, width_bins)
    chosen = tables[use_lists].reshape(block_count, USES * GROUP, width_bins)
    offsets = jnp.einsum(
        "bsk,bkn->bsn",
        loadings.reshape(block_count, BLOCK_STARS, USES * GROUP),
        chosen,
        preferred_element_type=jnp.float32,
    )
    corrected = (
        residuals.reshape(block_count, BLOCK_STARS, width_bins).astype(jnp.float32) - offsets
    ).astype(jnp.bfloat16)
    corrected = corrected.reshape(local_rows, width_bins)
    sketched = jnp.dot(corrected, sketch_matrix, preferred_element_type=jnp.float32)
    sketch_low = sketched.astype(jnp.bfloat16)
    devices_all = lax.axis_size(("rows", "units"))
    total_stars = local_rows * devices_all
    gram_local = jnp.dot(sketched.T, sketched, precision=lax.Precision.HIGHEST) / total_stars
    lower_factor = jnp.linalg.cholesky(lax.psum(gram_local, ("rows", "units")))
    star_basis = lax.linalg.triangular_solve(
        lower_factor, sketched, left_side=False, lower=True, transpose_a=True
    )
    bin_share = width_bins // devices_all
    full_terms = jnp.einsum("sn,sm->nm", corrected, sketch_low, preferred_element_type=jnp.float32)
    summed_all = lax.psum(full_terms, ("rows", "units"))
    first_bin = lax.axis_index(("rows", "units")) * bin_share
    summed = lax.dynamic_slice_in_dim(summed_all, first_bin, bin_share, 0)
    raw_modes = summed / total_stars
    bin_modes = lax.linalg.triangular_solve(
        lower_factor, raw_modes, left_side=False, lower=True, transpose_a=True
    )
    return (star_basis, bin_modes)


def solution(mesh):
    in_specs = (
        P(("rows", "units"), None),
        P(("rows", "units"), None),
        P("units", None),
        P(),
        P(("rows", "units"), None),
    )
    out_specs = (P(("rows", "units"), None), P(("rows", "units"), None))
    return jax.shard_map(
        on_device, mesh=mesh, in_specs=in_specs, out_specs=out_specs, check_vma=False
    )
```

profile of v0, /device:TPU:1, one launch (start us, length us, event | category | flops | bytes accessed | tf_op | source)
XLA Modules:
  0.0 364.4 jit_solution(14588423251606039512)
XLA Ops:
  7.2 0.7 all-gather.2.cloned.1.call-update
  8.0 0.7 compare_select_fusion
  8.9 52.1 %all-gather.2.cloned.1.call-done = bf16[1024,2048]{1,0:T(8,128)(2,1)} async-done(((bf16[256,2048]{1,0:T(8,128)(2,1)}), bf16[1024,2048]{1,0:T(8,128)(2,1)}) %all-gather.2.cloned.1.call-update) | async-done | bytes 4194320 | tf_op jit(solution)/shard_map/all_gather | solution.py:12
  60.9 14.9 %gather_fusion = bf16[128,64,2048]{2,1,0:T(8,128)(2,1)} fusion(bf16[16,64,2048]{2,1,0:T(8,128)(2,1)} %bitcast.51, s32[1024]{0:T(1024)S(1)} %pad_clamp_fusion), kind=kCustom, calls=%fused_computation | custom fusion | bytes 67109376 | tf_op jit(solution)/shard_map/gather | solution.py:17
  75.8 23.4 %fusion = bf16[32,128,2048]{2,1,0:T(8,128)(2,1)} fusion(bf16[32,128,2048]{2,1,0:T(8,128)(2,1)} %bitcast.53, bf16[32,128,256]{2,1,0:T(8,128)(2,1)S(1)} %bitcast.50, bf16[32,256,2048]{2,1,0:T(8,128)(2,1)} %bitcast.52), kind=kOutput, calls=%fused_computation.4 | convolution fusion | flops 4320133120 | bytes 69206016 | tf_op jit(solution)/shard_map/bsk,bkn->bsn/dot_general | solution.py:18
  99.3 10.3 %fusion.16 = f32[4096,256]{1,0:T(8,128)S(1)} fusion(bf16[4096,2048]{1,0:T(8,128)(2,1)} %bitcast.54, bf16[2048,256]{1,0:T(8,128)(2,1)S(1)} %copy-done.5), kind=kOutput, calls=%fused_computation.44 | convolution fusion | flops 4294967296 | bytes 22020096 | tf_op jit(solution)/shard_map/dot_general | solution.py:28
  109.6 0.2 copy-done.4
  109.8 6.3 %fusion.3 = f32[2048,256]{1,0:T(8,128)} fusion(bf16[4096,2048]{1,0:T(8,128)(2,1)S(1)} %bitcast.55, f32[4096,256]{1,0:T(8,128)S(1)} %fusion.16), kind=kOutput, calls=%fused_computation.9 | convolution fusion | flops 4296015872 | bytes 23068672 | tf_op jit(solution)/shard_map/sn,sm->nm/dot_general | solution.py:38
  116.1 7.4 %convolution_multiply_fusion = f32[256,256]{0,1:T(8,128)} fusion(f32[4096,256]{1,0:T(8,128)S(1)} %fusion.16), kind=kOutput, calls=%fused_computation.11 | convolution fusion | flops 3221291008 | bytes 4456448 | tf_op jit(solution)/shard_map/dot_general | solution.py:32
  123.6 152.5 %all-reduce.4.cloned.1.call-done = (f32[256,256]{0,1:T(8,128)}, f32[2048,256]{1,0:T(8,128)}) async-done(((f32[256,256]{0,1:T(8,128)}, f32[2048,256]{1,0:T(8,128)}), (f32[256,256]{0,1:T(8,128)}, f32[2048,256]{1,0:T(8,128)})) %all-reduce.4.cloned.1.call-update) | async-done | bytes 2359312 | tf_op jit(solution)/shard_map/psum | solution.py:33
  276.1 1.2 copy.13
  277.4 1.0 fusion.5
  278.4 11.7 %cholesky.50 = f32[128,128]{1,0:T(8,128)S(1)} custom-call(f32[128,128]{1,0:T(8,128)S(1)} %cholesky.118), custom_call_target="Cholesky" | custom-call | tf_op jit(solution)/shard_map/jit(cholesky)/cholesky | solution.py:33
  290.1 9.8 %custom-call.16 = f32[1,128,128]{1,2,0:T(8,128)S(1)} custom-call(f32[1,128,128]{2,1,0:T(8,128)S(1)} %get-tuple-element.29), custom_call_target="InvertDiagBlocksLowerTriangular" | custom-call | tf_op jit(solution)/shard_map/jit(cholesky)/cholesky | solution.py:33
  300.0 0.2 constant_dynamic-update-slice_fusion.1
  300.2 0.3 convolution_subtract_fusion.1
  300.5 11.7 %cholesky.105 = f32[128,128]{1,0:T(8,128)S(1)} custom-call(f32[128,128]{1,0:T(8,128)S(1)} %convolution_subtract_fusion.1), custom_call_target="Cholesky" | custom-call | tf_op jit(solution)/shard_map/jit(cholesky)/cholesky | solution.py:33
  312.2 0.7 compare_reduce_fusion
  314.3 3.9 %while.1 = (s32[]{:T(128)}, f32[256,256]{1,0:T(8,128)S(1)}, s32[2,2]{1,0:T(2,128)S(1)}, f32[2,128,128]{2,1,0:T(8,128)S(1)}, s32[]{:T(128)}) while((s32[]{:T(128)}, f32[256,256]{1,0:T(8,128)S(1)}, s32[2,2]{1,0:T(2,128)S(1)}, f32[2,128,128]{2,1,0:T(8,128)S(1)}, s32[]{:T(128)}) %tuple.29), condition=%wide.while_cond, body=%wide.while_body.sunk | while | flops 2 | bytes 131181 | solution.py:34
  314.3 0.6 fusion.31
  314.9 1.3 bitcast_dynamic-update-slice_fusion.2
  316.2 0.6 fusion.31
  316.8 1.3 bitcast_dynamic-update-slice_fusion.2
  318.1 19.9 %custom-call.17 = f32[2,128,128]{1,2,0:T(8,128)S(1)} custom-call(f32[2,128,128]{2,1,0:T(8,128)S(1)} %get-tuple-element.9), custom_call_target="InvertDiagBlocksLowerTriangular" | custom-call | tf_op jit(solution)/shard_map/triangular_solve | solution.py:34
  338.1 3.7 %fusion.1 = f32[4096,128]{0,1:T(8,128)S(1)} fusion(f32[4096,256]{1,0:T(8,128)} %copy-done.2, f32[2,128,128]{1,2,0:T(8,128)S(1)} %custom-call.17), kind=kOutput, calls=%fused_computation.7 | convolution fusion | flops 805306368 | bytes 4259840 | tf_op jit(solution)/shard_map/triangular_solve | solution.py:34
  341.8 0.7 dynamic-slice_multiply_fusion
  342.9 0.2 fusion.10
  343.1 0.6 pad_maximum_fusion.1
  343.7 3.6 convolution_subtract_fusion
  347.3 2.0 fusion.11
  349.3 2.4 pad_maximum_fusion
  351.7 5.6 %copy.14 = f32[4096,256]{1,0:T(8,128)} copy(f32[4096,256]{0,1:T(8,128)} %pad_maximum_fusion) | data formatting | bytes 8388608
  (29 shorter events, 0.9 us)
Async XLA Ops:
  7.2 68.7 %copy-start = (bf16[4096,256]{1,0:T(8,128)(2,1)S(1)}, bf16[4096,256]{1,0:T(8,128)(2,1)}, u32[]{:S(2)}) copy-start(bf16[4096,256]{1,0:T(8,128)(2,1)} %param.6) | copy-start | bytes 6291460
  7.2 53.8 %all-gather.2.cloned.1.call-start = ((), (), s32[]{:S(2)}) async-start(), calls=%async_computation | async-start | bytes 5242880 | tf_op jit(solution)/shard_map/all_gather | solution.py:12
  7.9 268.2 %all-reduce.4.cloned.1.call-start = ((), (), s32[]{:S(2)}) async-start(), calls=%async_computation.1 | async-start | bytes 4718592 | tf_op jit(solution)/shard_map/psum | solution.py:33
  75.8 23.4 %copy-start.5 = (bf16[2048,256]{1,0:T(8,128)(2,1)S(1)}, bf16[2048,256]{1,0:T(8,128)(2,1)}, u32[]{:S(2)}) copy-start(bf16[2048,256]{1,0:T(8,128)(2,1)} %param.8) | copy-start | bytes 3145732
  99.3 10.5 %copy-start.4 = (bf16[32,128,2048]{2,1,0:T(8,128)(2,1)S(1)}, bf16[32,128,2048]{2,1,0:T(8,128)(2,1)}, u32[]{:S(2)}) copy-start(bf16[32,128,2048]{2,1,0:T(8,128)(2,1)} %fusion) | copy-start | bytes 50331652
  109.8 6.3 %copy-start.2 = (f32[4096,256]{1,0:T(8,128)}, f32[4096,256]{1,0:T(8,128)S(1)}, u32[]{:S(2)}) copy-start(f32[4096,256]{1,0:T(8,128)S(1)} %fusion.16) | copy-start | bytes 12582916
  338.0 5.7 %copy-start.3 = (f32[4096,256]{1,0:T(8,128)S(1)}, f32[4096,256]{1,0:T(8,128)}, u32[]{:S(2)}) copy-start(f32[4096,256]{1,0:T(8,128)} %copy-done.2) | copy-start | bytes 12582916
  349.3 8.0 %copy-start.1 = (bf16[4096,256]{1,0:T(8,128)(2,1)S(1)}, bf16[4096,256]{1,0:T(8,128)(2,1)}, u32[]{:S(2)}) copy-start(bf16[4096,256]{1,0:T(8,128)(2,1)} %param.6) | copy-start | bytes 6291460
Sparse Core Ops, SparseCore 0:
  9.7 51.2 all-gather.1
  123.7 152.3 all-reduce.3
where the time goes:
time: 369 us; the launch traced here: 364 us
  waiting for transfers between devices  205 us (56%)
  other arithmetic  59.4 us (16%)
  matrix products  57.9 us (16%)
  local copies, waits for them, and re-layouts  26.1 us (7%)
  between operations  15.7 us (4%)
    psum x1, waiting for transfers between devices, on_device(): lower_factor = jnp.linalg.cholesky(lax.psum(gram_local, ('rows', 'units')))  153 us
    all_gather x1, waiting for transfers between devices, on_device(): gathered = lax.all_gather(zero_points, 'units', axis=0, tiled=True)  52.1 us
    another operation x6, other arithmetic, on_device(): lower_factor = jnp.linalg.cholesky(lax.psum(gram_local, ('rows', 'units')))  34 us
    dot_general x1, matrix products, on_device(): jnp.einsum('bsk,bkn->bsn', loadings.reshape(block_count, BLOCK_STARS, USE...  23.4 us
    another operation x4, other arithmetic, on_device(): lax.linalg.triangular_solve(lower_factor, sketched, left_side=False, lowe...  22.3 us
    gather x1, local copies, waits for them, and re-layouts, on_device(): chosen = tables[use_lists].reshape(block_count, USES * GROUP, width_bins)  14.9 us
    dot_general x1, matrix products, on_device(): jnp.dot(corrected, sketch_matrix, preferred_element_type=jnp.float32)  10.3 us
    another operation x3, matrix products, on_device(): lax.linalg.triangular_solve(lower_factor, sketched, left_side=False, lowe...  9.32 us
  transfers between devices with their start and end apart: 2, of which 2 were waited for; matrix products, arithmetic and copies ran while one was open for 0% of the time, Pallas kernels for 0%

commit v1 on v0

--- a/solution.py
+++ b/solution.py
@@ -30,7 +30,9 @@
     devices_all = lax.axis_size(("rows", "units"))
     total_stars = local_rows * devices_all
     gram_local = jnp.dot(sketched.T, sketched, precision=lax.Precision.HIGHEST) / total_stars
-    lower_factor = jnp.linalg.cholesky(lax.psum(gram_local, ("rows", "units")))
+    lower_factor = jnp.linalg.cholesky(
+        jnp.sum(jax.lax.all_gather(gram_local, axis_name=("rows", "units")), 0)
+    )
     star_basis = lax.linalg.triangular_solve(
         lower_factor, sketched, left_side=False, lower=True, transpose_a=True
     )

time: 369 us -> 482 us (1.31)
  waiting for transfers between devices: 205 us -> 300 us
  other arithmetic: 59.4 us -> 70.5 us
    all_gather x0 -> x1, waiting for transfers between devices: none -> 108 us  [on_device(): jax.lax.all_gather(gram_local, axis_name=('rows', 'units'))]
    psum x1, waiting for transfers between devices: 153 us -> 140 us  [on_device(): summed_all = lax.psum(full_terms, ('rows', 'units'))]
    reduce_sum x0 -> x1, other arithmetic: none -> 12.2 us  [on_device(): jnp.sum(jax.lax.all_gather(gram_local, axis_name=('rows', 'units')), 0)]
  transfers between devices with their start and end apart: 2 -> 3, of which waited for: 2 -> 3; matrix products, arithmetic and copies ran while one was open for 0% -> 3% of each run, Pallas kernels for 0% -> 0%
where the time goes in v1:
time: 482 us; the launch traced here: 475 us
  waiting for transfers between devices  300 us (62%)
  other arithmetic  70.5 us (15%)
  matrix products  61 us (13%)
  local copies, waits for them, and re-layouts  26.8 us (6%)
  between operations  15.4 us (3%)
    psum x1, waiting for transfers between devices, on_device(): summed_all = lax.psum(full_terms, ('rows', 'units'))  140 us
    all_gather x1, waiting for transfers between devices, on_device(): jax.lax.all_gather(gram_local, axis_name=('rows', 'units'))  108 us
    all_gather x1, waiting for transfers between devices, on_device(): gathered = lax.all_gather(zero_points, 'units', axis=0, tiled=True)  52.1 us
    another operation x6, other arithmetic, on_device(): jnp.linalg.cholesky(jnp.sum(jax.lax.all_gather(gram_local, axis_name=('ro...  34 us
    dot_general x1, matrix products, on_device(): jnp.einsum('bsk,bkn->bsn', loadings.reshape(block_count, BLOCK_STARS, USE...  23.4 us
    another operation x4, other arithmetic, on_device(): lax.linalg.triangular_solve(lower_factor, sketched, left_side=False, lowe...  22.3 us
    gather x1, local copies, waits for them, and re-layouts, on_device(): chosen = tables[use_lists].reshape(block_count, USES * GROUP, width_bins)  14.9 us
    reduce_sum x1, other arithmetic, on_device(): jnp.sum(jax.lax.all_gather(gram_local, axis_name=('rows', 'units')), 0)  12.2 us
  transfers between devices with their start and end apart: 3, of which 3 were waited for; matrix products, arithmetic and copies ran while one was open for 3% of the time, Pallas kernels for 0%

profile of v1, /device:TPU:1, one launch (start us, length us, event | category | flops | bytes accessed | tf_op | source)
XLA Modules:
  0.0 474.8 jit_solution(12183699995980723788)
XLA Ops:
  7.2 0.7 all-gather.4.cloned.1.call-update
  8.0 0.7 compare_select_fusion
  8.9 52.1 %all-gather.4.cloned.1.call-done = bf16[1024,2048]{1,0:T(8,128)(2,1)} async-done(((bf16[256,2048]{1,0:T(8,128)(2,1)}), bf16[1024,2048]{1,0:T(8,128)(2,1)}) %all-gather.4.cloned.1.call-update) | async-done | bytes 4194320 | tf_op jit(solution)/shard_map/all_gather | solution.py:12
  60.9 14.9 %gather_fusion = bf16[128,64,2048]{2,1,0:T(8,128)(2,1)} fusion(bf16[16,64,2048]{2,1,0:T(8,128)(2,1)} %bitcast.52, s32[1024]{0:T(1024)S(1)} %pad_clamp_fusion), kind=kCustom, calls=%fused_computation | custom fusion | bytes 67109376 | tf_op jit(solution)/shard_map/gather | solution.py:17
  75.8 23.4 %fusion = bf16[32,128,2048]{2,1,0:T(8,128)(2,1)} fusion(bf16[32,128,2048]{2,1,0:T(8,128)(2,1)} %bitcast.55, bf16[32,128,256]{2,1,0:T(8,128)(2,1)S(1)} %bitcast.51, bf16[32,256,2048]{2,1,0:T(8,128)(2,1)} %bitcast.53), kind=kOutput, calls=%fused_computation.4 | convolution fusion | flops 4320133120 | bytes 69206016 | tf_op jit(solution)/shard_map/bsk,bkn->bsn/dot_general | solution.py:18
  99.3 9.9 %fusion.16 = f32[4096,256]{1,0:T(8,128)S(1)} fusion(bf16[4096,2048]{1,0:T(8,128)(2,1)} %bitcast.56, bf16[2048,256]{1,0:T(8,128)(2,1)S(1)} %copy-done.5), kind=kOutput, calls=%fused_computation.44 | convolution fusion | flops 4294967296 | bytes 22020096 | tf_op jit(solution)/shard_map/dot_general | solution.py:28
  109.2 2.0 copy-done.2
  111.2 6.4 %fusion.3 = f32[2048,256]{1,0:T(8,128)} fusion(bf16[4096,2048]{1,0:T(8,128)(2,1)S(1)} %bitcast.57, f32[4096,256]{1,0:T(8,128)S(1)} %fusion.16), kind=kOutput, calls=%fused_computation.9 | convolution fusion | flops 4296015872 | bytes 23068672 | tf_op jit(solution)/shard_map/sn,sm->nm/dot_general | solution.py:40
  117.6 0.5 all-gather.6.cloned.1.call-start
  118.1 10.9 %convolution_multiply_fusion = f32[256,256]{1,0:T(8,128)} fusion(f32[4096,256]{1,0:T(8,128)} %copy-done.2), kind=kOutput, calls=%fused_computation.11 | convolution fusion | flops 3221291008 | bytes 4456448 | tf_op jit(solution)/shard_map/dot_general | solution.py:32
  129.1 140.1 %all-reduce.3.cloned.1.call-done = f32[2048,256]{1,0:T(8,128)} async-done(((f32[2048,256]{1,0:T(8,128)}), f32[2048,256]{1,0:T(8,128)}) %all-reduce.3.cloned.1.call-update) | async-done | bytes 2097168 | tf_op jit(solution)/shard_map/psum | solution.py:41
  269.2 0.7 dynamic-slice_multiply_fusion
  269.9 107.6 %all-gather.6.cloned.1.call-done = f32[32768,256]{1,0:T(8,128)} async-done(((f32[256,256]{1,0:T(8,128)}), f32[32768,256]{1,0:T(8,128)}) %all-gather.6.cloned.1.call-update) | async-done | bytes 33554448 | tf_op jit(solution)/shard_map/all_gather | solution.py:34
  377.5 12.2 %reduce_sum.9 = f32[256,256]{1,0:T(8,128)S(1)} reduce(f32[128,256,256]{2,1,0:T(8,128)} %bitcast.54, f32[]{:T(128)} %constant.97.clone.1), dimensions={0}, to_apply=%region_0.0 | reduce | flops 8323072 | bytes 33816580 | tf_op jit(solution)/shard_map/reduce_sum | solution.py:34
  389.8 11.7 %cholesky.50 = f32[128,128]{1,0:T(8,128)S(1)} custom-call(f32[128,128]{1,0:T(8,128)S(1)} %cholesky.118), custom_call_target="Cholesky" | custom-call | tf_op jit(solution)/shard_map/jit(cholesky)/cholesky | solution.py:33
  401.6 9.8 %custom-call.16 = f32[1,128,128]{1,2,0:T(8,128)S(1)} custom-call(f32[1,128,128]{2,1,0:T(8,128)S(1)} %get-tuple-element.29), custom_call_target="InvertDiagBlocksLowerTriangular" | custom-call | tf_op jit(solution)/shard_map/jit(cholesky)/cholesky | solution.py:33
  411.4 0.2 constant_dynamic-update-slice_fusion.1
  411.6 0.3 convolution_subtract_fusion.1
  411.9 11.7 %cholesky.105 = f32[128,128]{1,0:T(8,128)S(1)} custom-call(f32[128,128]{1,0:T(8,128)S(1)} %convolution_subtract_fusion.1), custom_call_target="Cholesky" | custom-call | tf_op jit(solution)/shard_map/jit(cholesky)/cholesky | solution.py:33
  423.6 0.7 compare_reduce_fusion
  425.7 3.9 while.1
  425.7 0.6 fusion.31
  426.3 1.3 bitcast_dynamic-update-slice_fusion.2
  427.6 0.6 fusion.31
  428.2 1.3 bitcast_dynamic-update-slice_fusion.2
  429.6 19.9 %custom-call.17 = f32[2,128,128]{1,2,0:T(8,128)S(1)} custom-call(f32[2,128,128]{2,1,0:T(8,128)S(1)} %get-tuple-element.9), custom_call_target="InvertDiagBlocksLowerTriangular" | custom-call | tf_op jit(solution)/shard_map/triangular_solve | solution.py:36
  449.5 3.7 fusion.1
  453.8 0.6 pad_maximum_fusion.1
  454.4 3.6 convolution_subtract_fusion
  458.0 2.0 fusion.11
  460.0 2.4 pad_maximum_fusion
  462.4 5.6 %copy.15 = f32[4096,256]{1,0:T(8,128)} copy(f32[4096,256]{0,1:T(8,128)} %pad_maximum_fusion) | data formatting | bytes 8388608
  (33 shorter events, 1.3 us)
Async XLA Ops:
  7.2 68.7 %copy-start = (bf16[4096,256]{1,0:T(8,128)(2,1)S(1)}, bf16[4096,256]{1,0:T(8,128)(2,1)}, u32[]{:S(2)}) copy-start(bf16[4096,256]{1,0:T(8,128)(2,1)} %param.6) | copy-start | bytes 6291460
  7.2 53.8 %all-gather.4.cloned.1.call-start = ((), (), s32[]{:S(2)}) async-start(), calls=%async_computation | async-start | bytes 5242880 | tf_op jit(solution)/shard_map/all_gather | solution.py:12
  7.9 261.3 %all-reduce.3.cloned.1.call-start = ((), (), s32[]{:S(2)}) async-start(), calls=%async_computation.1 | async-start | bytes 4194304 | tf_op jit(solution)/shard_map/psum | solution.py:41
  75.8 23.4 %copy-start.5 = (bf16[2048,256]{1,0:T(8,128)(2,1)S(1)}, bf16[2048,256]{1,0:T(8,128)(2,1)}, u32[]{:S(2)}) copy-start(bf16[2048,256]{1,0:T(8,128)(2,1)} %param.8) | copy-start | bytes 3145732
  99.3 11.9 %copy-start.4 = (bf16[32,128,2048]{2,1,0:T(8,128)(2,1)S(1)}, bf16[32,128,2048]{2,1,0:T(8,128)(2,1)}, u32[]{:S(2)}) copy-start(bf16[32,128,2048]{2,1,0:T(8,128)(2,1)} %fusion) | copy-start | bytes 50331652
  109.2 2.0 copy-start.2
  117.6 259.9 %all-gather.6.cloned.1.call-start = ((), (), s32[]{:S(2)}) async-start(), calls=%async_computation.2 | async-start | bytes 33816576 | tf_op jit(solution)/shard_map/all_gather | solution.py:34
  449.5 4.9 %copy-start.3 = (f32[4096,256]{1,0:T(8,128)S(1)}, f32[4096,256]{1,0:T(8,128)}, u32[]{:S(2)}) copy-start(f32[4096,256]{1,0:T(8,128)} %copy-done.2) | copy-start | bytes 12582916
  460.0 8.0 %copy-start.1 = (bf16[4096,256]{1,0:T(8,128)(2,1)S(1)}, bf16[4096,256]{1,0:T(8,128)(2,1)}, u32[]{:S(2)}) copy-start(bf16[4096,256]{1,0:T(8,128)(2,1)} %param.6) | copy-start | bytes 6291460
Sparse Core Ops, SparseCore 0:
  9.7 51.2 all-gather.3
  117.7 151.4 all-reduce.2
  272.4 105.0 all-gather.5
